TPU v7x, 128 devices: a whole 4x4x4 slice. The times are simulated.
128 devices in a mesh: lat: 16 (over z, x), lon: 8 (over y, core).
Axes of the slice: x: 4, y: 4, z: 4, core: 2. Of those that a mesh axis runs over, the one named last changes fastest.
Arguments:
- parent: bfloat16 [256, 256, 512], P('lat', 'lon'), may hold values from -6 to 6
- diffusion: float32 [512], replicated, may hold values from 0.05 to 0.25
- nest_state: bfloat16 [32768, 8, 512], P(('lat', 'lon')), may hold values from -6 to 6
- nest_cotangent: bfloat16 [32768, 8, 512], P(('lat', 'lon')), may hold values from -6 to 6
- owner_count: int32 [128], P(('lat', 'lon')), may hold values from 0 to 256, as said below
- tile_pos: int32 [32768], P(('lat', 'lon')), may hold values from 0 to 511
- w_in: bfloat16 [512, 2048], replicated, may hold values from -0.25 to 0.25
- w_out: bfloat16 [2048, 512], replicated, may hold values from -0.125 to 0.125
Outputs:
- parent_out: bfloat16 [256, 256, 512], P('lat', 'lon')
- nest_grad: bfloat16 [32768, 8, 512], P(('lat', 'lon'))
- w_in_grad: float32 [512, 2048], replicated
- w_out_grad: float32 [2048, 512], replicated
Inputs may be any that keep to these rules, and one draw needn't show every extreme that they name: `owner_count`: the counts of all devices sum to 8192; each is a multiple of 2; some device has exactly 256. Only the first count slots of a device are live; the entries of its other slots are not used.
All inputs are finite; a program needn't handle non-finite values.
Results may differ from a plain program's by a relative error of at most 0.012.
Values may be sent and summed in bfloat16 or wider, within the bound.
A program may use at most 128 MiB of HBM per device.

v0:
```python
import math

import jax
import jax.numpy as jnp
from jax import lax
from jax.sharding import PartitionSpec as P


def extended(x, sides, width, wrap):
    for axis, dim in sides:
        size, length = (lax.axis_size(axis), x.shape[dim])
        up = [(i, (i + 1) % size) for i in range(size if wrap else size - 1)]
        down = [(j, i) for i, j in up]
        last = lax.slice_in_dim(x, length - width, length, axis=dim)
        leading = lax.slice_in_dim(x, 0, width, axis=dim)
        before = lax.ppermute(last, axis, up)
        after = lax.ppermute(leading, axis, down)
        x = jnp.concatenate([before, x, after], axis=dim)
    return x


def nest_block(inputs, cotangent, w_in, w_out):
    count, cells, chans = inputs.shape
    rows = inputs.reshape(count * cells, chans)
    grads = cotangent.reshape(count * cells, chans)
    hidden = jnp.dot(rows, w_in, preferred_element_type=jnp.float32)
    active = jax.nn.gelu(hidden).astype(jnp.bfloat16)
    output = rows.astype(jnp.float32) + jnp.dot(active, w_out, preferred_element_type=jnp.float32)
    feedback = jnp.mean(output.reshape(count, cells, chans), axis=1).astype(jnp.bfloat16)
    d_active = jnp.dot(grads, w_out.T, preferred_element_type=jnp.float32)
    d_hidden = jax.vjp(jax.nn.gelu, hidden)[1](d_active)[0].astype(jnp.bfloat16)
    d_inputs = (
        grads.astype(jnp.float32) + jnp.dot(d_hidden, w_in.T, preferred_element_type=jnp.float32)
    ).astype(jnp.bfloat16)
    grad_in = jnp.dot(rows.T, d_hidden, preferred_element_type=jnp.float32)
    grad_out = jnp.dot(active.T, grads, preferred_element_type=jnp.float32)
    return (d_inputs.reshape(count, cells, chans), feedback, grad_in, grad_out)


def local(parent, diffusion, nest_state, nest_cotangent, owner_count, tile_pos, w_in, w_out):
    blat, blon, chans = parent.shape
    own_tiles, tile_rows = (nest_state.shape[0], nest_state.shape[1])
    lat_pad = extended(parent, (("lat", 0),), 1, False).astype(jnp.float32)
    lon_pad = extended(parent, (("lon", 1),), 1, True).astype(jnp.float32)
    field = parent.astype(jnp.float32)
    beside_all = lat_pad[2:] + lat_pad[:-2] + lon_pad[:, 2:] + lon_pad[:, :-2] - 4.0 * field
    smoothed = field + diffusion * beside_all
    flat = smoothed.reshape(blat * blon, chans)
    context = jnp.take(flat, tile_pos, axis=0)
    inputs = (nest_state.astype(jnp.float32) + context[:, None, :]).astype(jnp.bfloat16)
    live = lax.iota(jnp.int32, own_tiles) < owner_count[0]
    cotangent = jnp.where(live[:, None, None], nest_cotangent, jnp.zeros_like(nest_cotangent))
    devices = lax.axis_size(("lat", "lon"))
    d_inputs, feedback, grad_in, grad_out = nest_block(inputs, cotangent, w_in, w_out)
    nest_grad = jnp.where(live[:, None, None], d_inputs, jnp.zeros_like(d_inputs))
    feedback_live = jnp.where(live[:, None], feedback.astype(jnp.float32), 0.0)
    onehot = (tile_pos[:, None] == lax.iota(jnp.int32, blat * blon)[None, :]).astype(jnp.float32)
    summed = jnp.dot(onehot.T, feedback_live, precision=lax.Precision.HIGHEST)
    parent_out = (smoothed + summed.reshape(blat, blon, chans)).astype(jnp.bfloat16)
    factor = 1.0 / math.sqrt(own_tiles * devices // 4 * tile_rows)
    grad_in, grad_out = (
        lax.psum((grad_in * factor).astype(jnp.bfloat16), ("lat", "lon")).astype(jnp.float32),
        lax.psum((grad_out * factor).astype(jnp.bfloat16), ("lat", "lon")).astype(jnp.float32),
    )
    return (parent_out, nest_grad, grad_in, grad_out)


def solution(mesh):
    in_specs = (
        P("lat", "lon", None),
        P(),
        P(("lat", "lon"), None, None),
        P(("lat", "lon"), None, None),
        P(("lat", "lon")),
        P(("lat", "lon")),
        P(),
        P(),
    )
    out_specs = (P("lat", "lon", None), P(("lat", "lon"), None, None), P(), P())
    return jax.shard_map(local, mesh=mesh, in_specs=in_specs, out_specs=out_specs, check_vma=False)
```

profile of v0, /device:TPU:1, one launch (start us, length us, event | category | flops | bytes accessed | tf_op | source)
XLA Modules:
  0.0 245.0 jit_solution(15715763716594859502)
XLA Ops:
  7.2 0.0 copy-start
  7.2 0.0 all-reduce.3.cloned.1.call-start
  7.2 0.0 copy-start.1
  7.2 1.2 fusion.25
  8.4 1.4 collective-permute-start.3
  9.8 1.3 collective-permute-start.2
  11.1 0.8 fusion.24
  11.9 1.3 collective-permute-start.1
  13.2 4.0 %collective-permute-start = (bf16[1,32,512]{2,1,0:T(8,128)(2,1)S(1)}, bf16[1,32,512]{2,1,0:T(8,128)(2,1)S(1)}, u32[]{:S(2)}, u32[]{:S(2)}) collective-permute-start(bf16[1,32,512]{2,1,0:T(8,128)(2,1)S(1)} %get-tuple-element.6), channel_id=1, source_target_pairs={{0,8},{8,16},{16,24},{24,32},{32,40},{40,48},{48,56},{56,64},{64,7... | collective-permute-start | bytes 98312 | tf_op jit(solution)/shard_map/ppermute | solution.py:16
  17.2 0.7 compare_select_fusion
  17.9 0.7 compare_and_fusion
  19.2 0.0 collective-permute-done.3
  19.2 0.0 collective-permute-done.2
  19.3 1.3 maximum_convert_fusion
  20.5 0.0 collective-permute-done.1
  20.5 0.0 collective-permute-done
  20.6 1.1 maximum_convert_fusion.1
  21.7 0.0 copy-done.1
  21.7 1.1 convert_add_fusion
  22.8 1.8 gather_fusion
  24.5 1.1 broadcast_select_fusion.1
  25.7 0.0 copy-done
  25.7 0.0 copy-start.3
  25.7 0.0 copy-start.6
  25.7 0.0 copy-start.7
  25.7 14.4 %multiply_convert_fusion = (bf16[2048,2048]{1,0:T(8,128)(2,1)}, f32[2048,2048]{1,0:T(8,128)}) fusion(bf16[512,2048]{1,0:T(8,128)(2,1)S(1)} %copy-done, bf16[256,8,512]{2,1,0:T(8,128)(2,1)} %param.10, f32[256,512]{1,0:T(8,128)S(1)} %broadcast_select_fusion.1), kind=kOutput, calls=%fused_computation.10 | convolution fusion | flops 4335861760 | bytes 29884416 | tf_op jit(solution)/shard_map/dot_general | solution.py:26
  40.1 0.0 copy-done.6
  40.1 0.0 copy-done.7
  40.1 16.5 %fusion.6 = bf16[2048,2048]{1,0:T(8,128)(2,1)S(1)} fusion(f32[2048,2048]{1,0:T(8,128)} %get-tuple-element.11, bf16[2048,512]{1,0:T(8,128)(2,1)S(1)} %copy-done.6, bf16[256,8,512]{2,1,0:T(8,128)(2,1)S(1)} %copy-done.7, pred[256]{0:T(512)(128)(4,1)S(1)} %iota_compare_fusion.2), kind=kOutput, calls=%fused_computation.9 | convolution fusion | flops 4379901952 | bytes 29360384 | tf_op jit(solution)/shard_map/dot_general | solution.py:30
  56.7 0.0 copy-done.3
  56.7 0.0 copy-done.5
  56.7 0.0 copy-start.9
  56.7 5.9 %multiply_convert_fusion.2 = bf16[512,2048]{1,0:T(8,128)(2,1)} fusion(bf16[2048,2048]{1,0:T(8,128)(2,1)S(1)} %fusion.6, bf16[256,8,512]{2,1,0:T(8,128)(2,1)S(1)} %copy-done.5, f32[256,512]{1,0:T(8,128)S(1)} %broadcast_select_fusion.1), kind=kOutput, calls=%fused_computation.13 | convolution fusion | flops 4300210176 | bytes 13107200 | tf_op jit(solution)/shard_map/dot_general | solution.py:35
  62.6 0.0 copy-done.9
  62.6 9.4 %multiply_convert_fusion.1 = bf16[2048,512]{1,0:T(8,128)(2,1)} fusion(bf16[2048,2048]{1,0:T(8,128)(2,1)} %get-tuple-element.10, bf16[256,8,512]{2,1,0:T(8,128)(2,1)S(1)} %copy-done.7, pred[256]{0:T(512)(128)(4,1)S(1)} %iota_compare_fusion.2), kind=kOutput, calls=%fused_computation.12 | convolution fusion | flops 4298113024 | bytes 12583168 | tf_op jit(solution)/shard_map/dot_general | solution.py:36
  72.0 0.0 all-reduce.3.cloned.1.call-update
  72.1 0.0 copy-start.4
  72.1 10.4 %bitcast_reduce_fusion = f32[256,512]{1,0:T(8,128)S(1)} fusion(bf16[2048,2048]{1,0:T(8,128)(2,1)} %get-tuple-element.10, bf16[2048,512]{1,0:T(8,128)(2,1)} %param.15, f32[256,512]{1,0:T(8,128)} %copy-done.3, bf16[256,8,512]{2,1,0:T(8,128)(2,1)} %param.10), kind=kOutput, calls=%fused_computation.11 | convolution fusion | flops 4301127680 | bytes 13631488 | tf_op jit(solution)/shard_map/dot_general | solution.py:28
  82.4 0.0 copy-done.4
  82.4 0.0 copy-start.8
  82.5 0.8 fusion.15
  83.2 1.0 add_convert_fusion.2
  84.2 0.0 copy-done.8
  84.2 10.2 %bitcast_select_fusion = bf16[256,8,512]{2,1,0:T(8,128)(2,1)} fusion(pred[256]{0:T(512)(128)(4,1)S(1)} %iota_compare_fusion.2, bf16[2048,2048]{1,0:T(8,128)(2,1)} %copy-done.9, bf16[512,2048]{1,0:T(8,128)(2,1)S(1)} %copy-done, bf16[256,8,512]{2,1,0:T(8,128)(2,1)S(1)} %copy-done.8), kind=kOutput, calls=%fused_computation.17 | convolution fusion | flops 4300210176 | bytes 14680320 | tf_op jit(solution)/shard_map/dot_general | solution.py:33
  94.4 136.8 %all-reduce.3.cloned.1.call-done = (bf16[512,2048]{1,0:T(8,128)(2,1)}, bf16[2048,512]{1,0:T(8,128)(2,1)}) async-done(((bf16[512,2048]{1,0:T(8,128)(2,1)}, bf16[2048,512]{1,0:T(8,128)(2,1)}), (bf16[512,2048]{1,0:T(8,128)(2,1)}, bf16[2048,512]{1,0:T(8,128)(2,1)})) %all-reduce.3.cloned.1.call-update) | async-done | bytes 4194320 | tf_op jit(solution)/shard_map/psum | solution.py:62
  231.2 4.3 %convert_element_type.66 = f32[512,2048]{1,0:T(8,128)} convert(bf16[512,2048]{1,0:T(8,128)(2,1)} %get-tuple-element.4) | non-fusion elementwise | flops 1048576 | bytes 6291456 | tf_op jit(solution)/shard_map/convert_element_type | solution.py:62
  235.5 0.0 copy-done.2
  235.5 2.6 %convert_element_type.68 = f32[2048,512]{1,0:T(8,128)} convert(bf16[2048,512]{1,0:T(8,128)(2,1)S(1)} %copy-done.2) | non-fusion elementwise | flops 1048576 | bytes 6291456 | tf_op jit(solution)/shard_map/convert_element_type | solution.py:63
  (4 shorter events, 0.0 us)
Async XLA Ops:
  7.2 18.5 %copy-start = (bf16[512,2048]{1,0:T(8,128)(2,1)S(1)}, bf16[512,2048]{1,0:T(8,128)(2,1)}, u32[]{:S(2)}) copy-start(bf16[512,2048]{1,0:T(8,128)(2,1)} %param.14) | copy-start | bytes 6291460
  7.2 224.1 %all-reduce.3.cloned.1.call-start = ((), (), s32[]{:S(2)}) async-start(), calls=%async_computation | async-start | bytes 8388608 | tf_op jit(solution)/shard_map/psum | solution.py:62
  7.2 14.5 %copy-start.1 = (bf16[16,32,512]{2,1,0:T(8,128)(2,1)S(1)}, bf16[16,32,512]{2,1,0:T(8,128)(2,1)}, u32[]{:S(2)}) copy-start(bf16[16,32,512]{2,1,0:T(8,128)(2,1)} %param.8) | copy-start | bytes 1572868
  8.4 10.8 %collective-permute-start.3 = (bf16[16,1,512]{2,1,0:T(2,128)(2,1)S(1)}, bf16[16,1,512]{2,1,0:T(2,128)(2,1)S(1)}, u32[]{:S(2)}, u32[]{:S(2)}) collective-permute-start(bf16[16,1,512]{2,1,0:T(2,128)(2,1)S(1)} %get-tuple-element.9), channel_id=1, source_target_pairs={{1,0},{2,1},{3,2},{4,3},{5,4},{6,5},{7,6},{0,7},{9,8},{10,9},{11,1... | collective-permute-start | bytes 49160 | tf_op jit(solution)/shard_map/ppermute | solution.py:17
  9.8 9.4 %collective-permute-start.2 = (bf16[16,1,512]{2,1,0:T(2,128)(2,1)S(1)}, bf16[16,1,512]{2,1,0:T(2,128)(2,1)S(1)}, u32[]{:S(2)}, u32[]{:S(2)}) collective-permute-start(bf16[16,1,512]{2,1,0:T(2,128)(2,1)S(1)} %get-tuple-element.8), channel_id=1, source_target_pairs={{0,1},{1,2},{2,3},{3,4},{4,5},{5,6},{6,7},{7,0},{8,9},{9,10},{10,1... | collective-permute-start | bytes 49160 | tf_op jit(solution)/shard_map/ppermute | solution.py:16
  11.9 8.6 %collective-permute-start.1 = (bf16[1,32,512]{2,1,0:T(8,128)(2,1)S(1)}, bf16[1,32,512]{2,1,0:T(8,128)(2,1)S(1)}, u32[]{:S(2)}, u32[]{:S(2)}) collective-permute-start(bf16[1,32,512]{2,1,0:T(8,128)(2,1)S(1)} %get-tuple-element.7), channel_id=1, source_target_pairs={{8,0},{16,8},{24,16},{32,24},{40,32},{48,40},{56,48},{64,56},{72,6... | collective-permute-start | bytes 98312 | tf_op jit(solution)/shard_map/ppermute | solution.py:17
  13.2 7.4 %collective-permute-start = (bf16[1,32,512]{2,1,0:T(8,128)(2,1)S(1)}, bf16[1,32,512]{2,1,0:T(8,128)(2,1)S(1)}, u32[]{:S(2)}, u32[]{:S(2)}) collective-permute-start(bf16[1,32,512]{2,1,0:T(8,128)(2,1)S(1)} %get-tuple-element.6), channel_id=1, source_target_pairs={{0,8},{8,16},{16,24},{24,32},{32,40},{40,48},{48,56},{56,64},{64,7... | collective-permute-start | bytes 98312 | tf_op jit(solution)/shard_map/ppermute | solution.py:16
  25.7 31.0 %copy-start.3 = (f32[256,512]{1,0:T(8,128)}, f32[256,512]{1,0:T(8,128)S(1)}, u32[]{:S(2)}) copy-start(f32[256,512]{1,0:T(8,128)S(1)} %broadcast_select_fusion.1) | copy-start | bytes 1572868
  25.7 14.4 %copy-start.6 = (bf16[2048,512]{1,0:T(8,128)(2,1)S(1)}, bf16[2048,512]{1,0:T(8,128)(2,1)}, u32[]{:S(2)}) copy-start(bf16[2048,512]{1,0:T(8,128)(2,1)} %param.15) | copy-start | bytes 6291460
  25.7 14.4 %copy-start.7 = (bf16[256,8,512]{2,1,0:T(8,128)(2,1)S(1)}, bf16[256,8,512]{2,1,0:T(8,128)(2,1)}, u32[]{:S(2)}) copy-start(bf16[256,8,512]{2,1,0:T(8,128)(2,1)} %param.11) | copy-start | bytes 6291460
  40.1 16.5 %copy-start.5 = (bf16[256,8,512]{2,1,0:T(8,128)(2,1)S(1)}, bf16[256,8,512]{2,1,0:T(8,128)(2,1)}, u32[]{:S(2)}) copy-start(bf16[256,8,512]{2,1,0:T(8,128)(2,1)} %param.10) | copy-start | bytes 6291460
  56.7 5.9 %copy-start.9 = (bf16[2048,2048]{1,0:T(8,128)(2,1)}, bf16[2048,2048]{1,0:T(8,128)(2,1)S(1)}, u32[]{:S(2)}) copy-start(bf16[2048,2048]{1,0:T(8,128)(2,1)S(1)} %fusion.6) | copy-start | bytes 25165828
  72.1 10.4 %copy-start.4 = (s32[256]{0:T(256)S(1)}, s32[256]{0:T(256)}, u32[]{:S(2)}) copy-start(s32[256]{0:T(256)} %param.13) | copy-start | bytes 3076
  82.4 1.8 copy-start.8
  231.2 4.3 %copy-start.2 = (bf16[2048,512]{1,0:T(8,128)(2,1)S(1)}, bf16[2048,512]{1,0:T(8,128)(2,1)}, u32[]{:S(2)}) copy-start(bf16[2048,512]{1,0:T(8,128)(2,1)} %get-tuple-element.5) | copy-start | bytes 6291460
Sparse Core Ops, SparseCore 0:
  72.2 158.9 all-reduce.2
where the time goes:
time: 246 us; the launch traced here: 245 us
  waiting for transfers between devices  137 us (56%)
  matrix products  67.6 us (27%)
  between operations  14.9 us (6%)
  other arithmetic  13.8 us (6%)
  starting transfers between devices  8.02 us (3%)
  local copies, waits for them, and re-layouts  3.77 us (2%)
    psum x1, waiting for transfers between devices, local(): lax.psum((grad_in * factor).astype(jnp.bfloat16), ('lat', 'lon'))  137 us
    dot_general x1, matrix products, nest_block(): d_active = jnp.dot(grads, w_out.T, preferred_element_type=jnp.float32)  16.5 us
    dot_general x1, matrix products, nest_block(): hidden = jnp.dot(rows, w_in, preferred_element_type=jnp.float32)  14.4 us
    dot_general x1, matrix products, nest_block(): jnp.dot(active, w_out, preferred_element_type=jnp.float32)  10.4 us
    dot_general x1, matrix products, nest_block(): jnp.dot(d_hidden, w_in.T, preferred_element_type=jnp.float32)  10.2 us
    dot_general x1, matrix products, nest_block(): grad_out = jnp.dot(active.T, grads, preferred_element_type=jnp.float32)  9.43 us
    dot_general x1, matrix products, nest_block(): grad_in = jnp.dot(rows.T, d_hidden, preferred_element_type=jnp.float32)  5.92 us
    ppermute x2, starting transfers between devices, extended(): before = lax.ppermute(last, axis, up)  5.31 us
  transfers between devices with their start and end apart: 5, of which 1 were waited for; matrix products, arithmetic and copies ran while one was open for 11% of the time, Pallas kernels for 0%

commit v1 on v0

v1 whole, which is shorter than its diff:
```python
import math

import jax
import jax.numpy as jnp
from jax import lax
from jax.experimental import pallas as pl
from jax.experimental.pallas import tpu as pltpu
from jax.sharding import PartitionSpec as P

MESH = pl.DeviceIdType.MESH
F32 = jnp.float32
BF16 = jnp.bfloat16
NT = (((1,), (1,)), ((), ()))
TN = (((0,), (0,)), ((), ()))
G0 = math.sqrt(2.0 / math.pi)
G1 = G0 * 0.044715
CH = 256
NCH = 8
VMEM = pl.BlockSpec(memory_space=pltpu.VMEM)
PLANE = [(a, b) for a in range(4) for b in range(4) if a or b]


def extended(x, sides, width, wrap):
    for axis, dim in sides:
        size, length = (lax.axis_size(axis), x.shape[dim])
        up = [(i, (i + 1) % size) for i in range(size if wrap else size - 1)]
        down = [(j, i) for i, j in up]
        last = lax.slice_in_dim(x, length - width, length, axis=dim)
        leading = lax.slice_in_dim(x, 0, width, axis=dim)
        before = lax.ppermute(last, axis, up)
        after = lax.ppermute(leading, axis, down)
        x = jnp.concatenate([before, x, after], axis=dim)
    return x


def gelu_pair(h, da):
    h2 = h * h
    s = 0.5 + 0.5 * jnp.tanh(h * (G0 + G1 * h2))
    act = h * s
    slope = s + act * (1.0 - s) * (2.0 * G0 + 6.0 * G1 * h2)
    return act.astype(BF16), (slope * da).astype(BF16)


def block_kernel(factor, x, cot, wi, wo, part, dx, fb, xT, act, dh):
    xT[...] = x[...].T

    def chunk(j, carry):
        cols = pl.ds(pl.multiple_of(j * CH, CH), CH)

        def tile(r, carry):
            rows = pl.ds(pl.multiple_of(r * 512, 512), 512)
            h = jnp.dot(x[rows, :], wi[:, cols], preferred_element_type=F32)
            da = lax.dot_general(cot[rows, :], wo[cols, :], NT, preferred_element_type=F32)
            a, d = gelu_pair(h, da)
            act[rows, cols] = a
            dh[rows, cols] = d
            return carry

        lax.fori_loop(0, 4, tile, 0)
        gi = jnp.dot(xT[...], dh[:, cols], preferred_element_type=F32) * factor
        for k in range(2):
            part[j, 0, 32 * k : 32 * k + 32] = gi[:, 128 * k : 128 * k + 128].astype(BF16).reshape(32, 16, 128)
        go = lax.dot_general(act[:, cols], cot[...], TN, preferred_element_type=F32) * factor
        for k in range(4):
            part[j, 1, 16 * k : 16 * k + 16] = go[:, 128 * k : 128 * k + 128].astype(BF16).reshape(16, 16, 128)
        return carry

    lax.fori_loop(0, NCH, chunk, 0)

    def rest(r, carry):
        rows = pl.ds(pl.multiple_of(r * 256, 256), 256)
        d = lax.dot_general(dh[rows, :], wi[...], NT, preferred_element_type=F32)
        dx[rows, :] = (d + cot[rows, :].astype(F32)).astype(BF16)
        o = jnp.dot(act[rows, :], wo[...], preferred_element_type=F32) + x[rows, :].astype(F32)
        fb[pl.ds(pl.multiple_of(r * 32, 32), 32), :] = jnp.mean(o.reshape(32, 8, 512), axis=1).astype(BF16)
        return carry

    lax.fori_loop(0, 8, rest, 0)


class Place:
    def __init__(self):
        a, b = lax.axis_index("lat"), lax.axis_index("lon")
        self.x, self.y, self.z = lax.rem(a, 4), b // 2, a // 4
        self.core = lax.rem(b, 2)

    def to(self, dx, dy, dz):
        x, y, z = lax.rem(self.x + dx, 4), lax.rem(self.y + dy, 4), lax.rem(self.z + dz, 4)
        return (z * 4 + x, y * 2 + self.core)

    def partner(self):
        return (self.z * 4 + self.x, self.y * 2 + 1 - self.core)

    def axis(self, a):
        ex, ez = (2 - a) // 2, a // 2
        ey = 1 - ex - ez
        return ((ex, ey, ez), self.x * ex + self.y * ey + self.z * ez)


class Reduce:
    def __init__(self, part, full, rc, half, ra, qb, rp, send, recv):
        self.part, self.full, self.rc, self.half = part, full, rc, half
        self.ra, self.qb, self.rp, self.send, self.recv = ra, qb, rp, send, recv
        self.at = Place()

    def sets(self, c):
        a0 = lax.rem(c, 3)
        (e0, q) = self.at.axis(a0)
        (e1, u) = self.at.axis(lax.rem(a0 + 1, 3))
        (e2, v) = self.at.axis(lax.rem(a0 + 2, 3))
        return e0, e1, e2, q, u, v

    def copy(self, src, dst, stage, c, device):
        pltpu.make_async_remote_copy(
            src_ref=src, dst_ref=dst, send_sem=self.send.at[stage, c], recv_sem=self.recv.at[stage, c],
            device_id=device, device_id_type=MESH,
        ).start()

    def wait(self, ref, stage, c):
        pltpu.make_async_copy(ref, ref, self.recv.at[stage, c]).wait()

    def greet(self):
        barrier = pltpu.get_barrier_semaphore()
        n = 1
        pl.semaphore_signal(barrier, inc=1, device_id=self.at.partner(), device_id_type=MESH)
        for dx in range(4):
            for dy in range(4):
                for dz in range(4):
                    if (dx or dy or dz) and not (dx and dy and dz):
                        pl.semaphore_signal(barrier, inc=1, device_id=self.at.to(dx, dy, dz), device_id_type=MESH)
                        n += 1
        pl.semaphore_wait(barrier, n)

    def s0(self, c):
        self.copy(self.part.at[c, 1 - self.at.core], self.rc.at[c], 0, c, self.at.partner())

    def s1(self, c):
        e0, e1, e2, q, u, v = self.sets(c)
        self.wait(self.rc.at[c], 0, c)
        self.half[c] = (self.part[c, self.at.core].astype(F32) + self.rc[c].astype(F32)).astype(BF16)
        for d in (1, 2, 3):
            to = lax.rem(q + d, 4)
            self.copy(self.half.at[c, pl.ds(to * 16, 16)], self.ra.at[c, d - 1], 1, c, self.at.to(*(d * e for e in e0)))

    def s2(self, c):
        e0, e1, e2, q, u, v = self.sets(c)
        self.wait(self.ra.at[c], 1, c)
        mine = pl.ds(q * 16, 16)
        total = self.part[c, self.at.core, mine].astype(F32) + self.rc[c, mine].astype(F32)
        for d in range(3):
            total += self.ra[c, d].astype(F32)
        self.qb[c] = total.astype(BF16)
        for o, (d1, d2) in enumerate(PLANE):
            to = lax.rem(u + d1, 4) * 4 + lax.rem(v + d2, 4)
            self.copy(self.qb.at[c, to], self.rp.at[c, o], 2, c, self.at.to(*(d1 * f + d2 * g for f, g in zip(e1, e2))))

    def s3(self, c):
        e0, e1, e2, q, u, v = self.sets(c)
        self.wait(self.rp.at[c], 2, c)
        total = self.qb[c, u * 4 + v].astype(F32)
        for o in range(15):
            total += self.rp[c, o].astype(F32)
        spot = self.full.at[c, self.at.core, q * 16 + u * 4 + v]
        spot[...] = total.astype(BF16)
        for d1, d2 in PLANE:
            self.copy(spot, spot, 3, c, self.at.to(*(d1 * f + d2 * g for f, g in zip(e1, e2))))

    def s4(self, c):
        e0, e1, e2, q, u, v = self.sets(c)
        self.wait(self.rp.at[c], 3, c)
        spot = self.full.at[c, self.at.core, pl.ds(q * 16, 16)]
        for d in (1, 2, 3):
            self.copy(spot, spot, 4, c, self.at.to(*(d * e for e in e0)))

    def s5(self, c):
        self.wait(self.ra.at[c], 4, c)
        spot = self.full.at[c, self.at.core]
        self.copy(spot, spot, 5, c, self.at.partner())

    def s6(self, c, gi, go):
        self.wait(self.full.at[c, 1 - self.at.core], 5, c)
        for k in range(2):
            cols = pl.ds(pl.multiple_of(c * CH + 128 * k, 128), 128)
            gi[:, cols] = self.full[c, 0, 32 * k : 32 * k + 32].reshape(512, 128)
        for k in range(4):
            rows = pl.ds(pl.multiple_of(c * CH, CH), CH)
            go[rows, 128 * k : 128 * k + 128] = self.full[c, 1, 16 * k : 16 * k + 16].reshape(256, 128)

    def drain(self, c):
        for stage, ref in enumerate((self.rc, self.ra, self.rp, self.rp, self.ra, self.rc)):
            pltpu.make_async_copy(ref.at[c], ref.at[c], self.send.at[stage, c]).wait()


def reduce_kernel(part, gi, go, *scratch):
    r = Reduce(part, *scratch)
    r.greet()
    for stage in (r.s0, r.s1, r.s2, r.s3, r.s4, r.s5, lambda c: r.s6(c, gi, go), r.drain):
        def body(c, carry, stage=stage):
            stage(c)
            return carry
        lax.fori_loop(0, NCH, body, 0)


def local(parent, diffusion, nest_state, nest_cotangent, owner_count, tile_pos, w_in, w_out):
    blat, blon, chans = parent.shape
    own_tiles, tile_rows = (nest_state.shape[0], nest_state.shape[1])
    rows = own_tiles * tile_rows
    hidden = w_in.shape[1]
    lat_pad = extended(parent, (("lat", 0),), 1, False).astype(F32)
    lon_pad = extended(parent, (("lon", 1),), 1, True).astype(F32)
    field = parent.astype(F32)
    beside_all = lat_pad[2:] + lat_pad[:-2] + lon_pad[:, 2:] + lon_pad[:, :-2] - 4.0 * field
    smoothed = field + diffusion * beside_all
    flat = smoothed.reshape(blat * blon, chans)
    context = jnp.take(flat, tile_pos, axis=0)
    inputs = (nest_state.astype(F32) + context[:, None, :]).astype(BF16).reshape(rows, chans)
    live = lax.iota(jnp.int32, own_tiles) < owner_count[0]
    cotangent = jnp.where(live[:, None, None], nest_cotangent, jnp.zeros_like(nest_cotangent)).reshape(rows, chans)
    devices = lax.axis_size(("lat", "lon"))
    factor = 1.0 / math.sqrt(own_tiles * devices // 4 * tile_rows)
    part, d_inputs, feedback = pl.pallas_call(
        lambda *refs: block_kernel(factor, *refs),
        out_shape=[
            jax.ShapeDtypeStruct((NCH, 2, 64, 16, 128), BF16),
            jax.ShapeDtypeStruct((rows, chans), BF16),
            jax.ShapeDtypeStruct((own_tiles, chans), BF16),
        ],
        in_specs=[VMEM] * 4,
        out_specs=[VMEM] * 3,
        scratch_shapes=[pltpu.VMEM((chans, rows), BF16), pltpu.VMEM((rows, hidden), BF16), pltpu.VMEM((rows, hidden), BF16)],
        compiler_params=pltpu.CompilerParams(vmem_limit_bytes=56 * 2**20),
        name="nest_block",
    )(inputs, cotangent, w_in, w_out)
    nest_grad = jnp.where(live[:, None, None], d_inputs.reshape(nest_state.shape), jnp.zeros_like(nest_state))
    onehot = ((tile_pos[:, None] == lax.iota(jnp.int32, blat * blon)[None, :]) & live[:, None]).astype(BF16)
    summed = jnp.dot(onehot.T, feedback, preferred_element_type=F32)
    parent_out = (smoothed + summed.reshape(blat, blon, chans)).astype(BF16)
    grad_in, grad_out = pl.pallas_call(
        reduce_kernel,
        out_shape=[jax.ShapeDtypeStruct(w_in.shape, BF16), jax.ShapeDtypeStruct(w_out.shape, BF16)],
        in_specs=[VMEM],
        out_specs=[VMEM] * 2,
        scratch_shapes=[
            pltpu.VMEM((NCH, 2, 64, 16, 128), BF16),
            pltpu.VMEM((NCH, 64, 16, 128), BF16),
            pltpu.VMEM((NCH, 64, 16, 128), BF16),
            pltpu.VMEM((NCH, 3, 16, 16, 128), BF16),
            pltpu.VMEM((NCH, 16, 16, 128), BF16),
            pltpu.VMEM((NCH, 15, 16, 128), BF16),
            pltpu.SemaphoreType.DMA((6, NCH)),
            pltpu.SemaphoreType.DMA((6, NCH)),
        ],
        compiler_params=pltpu.CompilerParams(collective_id=0, has_side_effects=True, vmem_limit_bytes=56 * 2**20),
        name="reduce_all",
    )(part)
    return (parent_out, nest_grad, grad_in.astype(F32), grad_out.astype(F32))


def solution(mesh):
    in_specs = (
        P("lat", "lon", None),
        P(),
        P(("lat", "lon"), None, None),
        P(("lat", "lon"), None, None),
        P(("lat", "lon")),
        P(("lat", "lon")),
        P(),
        P(),
    )
    out_specs = (P("lat", "lon", None), P(("lat", "lon"), None, None), P(), P())
    return jax.shard_map(local, mesh=mesh, in_specs=in_specs, out_specs=out_specs, check_vma=False)
```

time: 246 us -> 127 us (0.52)
  waiting for transfers between devices: 137 us -> 0.01 us
  Pallas kernels: 0 us -> 93.2 us
  matrix products: 67.6 us -> 1.4 us
  between operations: 14.9 us -> 1.41 us
  other arithmetic: 13.8 us -> 19.6 us
    psum x1 -> x0, waiting for transfers between devices: 137 us -> none  [local(): lax.psum((grad_in * factor).astype(jnp.bfloat16), ('lat', 'lon'))]
    pallas_call x0 -> x2, Pallas kernels: none -> 93.2 us  [the longest x1 47.7 us: local(): pl.pallas_call(reduce_kernel, out_shape=[jax.ShapeDtypeStruct(w_in.shape,...]
    dot_general x7 -> x1, matrix products: 67.6 us -> 1.4 us  [local(): summed = jnp.dot(onehot.T, feedback, preferred_element_type=F32)]
    reshape x0 -> x2, other arithmetic: none -> 6.5 us  [the longest x1 3.34 us: local(): (nest_state.astype(F32) + context[:, None, :]).astype(BF16)]
    select_n x0 -> x1, other arithmetic: none -> 3.1 us  [local(): jnp.where(live[:, None, None], d_inputs.reshape(nest_state.shape), jnp.ze...]
  transfers between devices with their start and end apart: 5 -> 4, of which waited for: 1 -> 0; matrix products, arithmetic and copies ran while one was open for 11% -> 5% of each run, Pallas kernels for 0% -> 0%
where the time goes in v1:
time: 127 us; the launch traced here: 126 us
  Pallas kernels  93.2 us (73%)
  other arithmetic  19.6 us (15%)
  starting transfers between devices  7.37 us (6%)
  local copies, waits for them, and re-layouts  3.07 us (2%)
  between operations  1.41 us (1%)
  matrix products  1.4 us (1%)
    pallas_call x1, Pallas kernels, local(): pl.pallas_call(reduce_kernel, out_shape=[jax.ShapeDtypeStruct(w_in.shape,...  47.7 us
    pallas_call x1, Pallas kernels, local(): pl.pallas_call(lambda *refs: block_kernel(factor, *refs), out_shape=[jax....  45.5 us
    convert_element_type x2, other arithmetic, local(): return (parent_out, nest_grad, grad_in.astype(F32), grad_out.astype(F32))  6.89 us
    ppermute x2, starting transfers between devices, extended(): before = lax.ppermute(last, axis, up)  6.07 us
    reshape x1, other arithmetic, local(): (nest_state.astype(F32) + context[:, None, :]).astype(BF16)  3.34 us
    reshape x1, other arithmetic, local(): jnp.where(live[:, None, None], nest_cotangent, jnp.zeros_like(nest_cotang...  3.16 us
    select_n x1, other arithmetic, local(): jnp.where(live[:, None, None], d_inputs.reshape(nest_state.shape), jnp.ze...  3.1 us
  transfers between devices with their start and end apart: 4, of which 0 were waited for; matrix products, arithmetic and copies ran while one was open for 5% of the time, Pallas kernels for 0%

profile of v1, /device:TPU:1, one launch (start us, length us, event | category | flops | bytes accessed | tf_op | source)
XLA Modules:
  0.0 126.1 jit_solution(15236573709238979815)
XLA Ops:
  0.6 0.8 fusion.8
  1.4 3.9 %collective-permute-start = (bf16[1,32,512]{2,1,0:T(8,128)(2,1)S(1)}, bf16[1,32,512]{2,1,0:T(8,128)(2,1)S(1)}, u32[]{:S(2)}, u32[]{:S(2)}) collective-permute-start(bf16[1,32,512]{2,1,0:T(8,128)(2,1)S(1)} %get-tuple-element.14), channel_id=1, source_target_pairs={{0,8},{8,16},{16,24},{24,32},{32,40},{40,48},{48,56},{56,64},{64,7... | collective-permute-start | bytes 98312 | tf_op jit(solution)/shard_map/ppermute | solution.py:30
  5.3 1.3 %collective-permute-start.1 = (bf16[1,32,512]{2,1,0:T(8,128)(2,1)S(1)}, bf16[1,32,512]{2,1,0:T(8,128)(2,1)S(1)}, u32[]{:S(2)}, u32[]{:S(2)}) collective-permute-start(bf16[1,32,512]{2,1,0:T(8,128)(2,1)S(1)} %get-tuple-element.15), channel_id=1, source_target_pairs={{8,0},{16,8},{24,16},{32,24},{40,32},{48,40},{56,48},{64,56},{72,6... | collective-permute-start | bytes 98312 | tf_op jit(solution)/shard_map/ppermute | solution.py:31
  6.6 1.0 fusion.9
  7.7 2.1 %collective-permute-start.2 = (bf16[16,1,512]{2,1,0:T(2,128)(2,1)S(1)}, bf16[16,1,512]{2,1,0:T(2,128)(2,1)S(1)}, u32[]{:S(2)}, u32[]{:S(2)}) collective-permute-start(bf16[16,1,512]{2,1,0:T(2,128)(2,1)S(1)} %get-tuple-element.16), channel_id=1, source_target_pairs={{0,1},{1,2},{2,3},{3,4},{4,5},{5,6},{6,7},{7,0},{8,9},{9,10},{10,1... | collective-permute-start | bytes 49160 | tf_op jit(solution)/shard_map/ppermute | solution.py:30
  9.8 0.0 collective-permute-start.3
  9.8 0.7 compare_and_fusion
  10.5 0.7 compare_select_fusion
  11.9 0.0 copy-start
  11.9 3.2 %select_bitcast_fusion.refs_1_ = bf16[2048,512]{1,0:T(8,128)(2,1)} fusion(bf16[256,8,512]{2,1,0:T(8,128)(2,1)} %param.11, pred[256]{0:T(512)(128)(4,1)S(1)} %iota_compare_fusion.1), kind=kLoop, calls=%fused_computation.4 | loop fusion | flops 1048576 | bytes 4194560 | tf_op jit(solution)/shard_map/reshape | solution.py:218
  15.0 0.0 copy-start.3
  15.0 0.0 collective-permute-done.2
  15.1 0.0 collective-permute-done.3
  15.1 0.0 copy-done
  15.1 0.2 maximum_convert_fusion
  15.3 0.0 collective-permute-done
  15.3 0.0 collective-permute-done.1
  15.3 0.1 maximum_convert_fusion.1
  15.4 0.3 copy-done.3
  15.7 0.4 convert_add_fusion
  16.1 1.0 gather_fusion
  17.1 0.1 broadcast_select_fusion
  17.2 3.3 %fusion.refs_0_ = bf16[2048,512]{1,0:T(8,128)(2,1)} fusion(bf16[256,8,512]{2,1,0:T(8,128)(2,1)} %param.10, f32[256,512]{1,0:T(8,128)S(1)} %broadcast_select_fusion), kind=kLoop, calls=%fused_computation.2 | loop fusion | flops 3145728 | bytes 4718592 | tf_op jit(solution)/shard_map/reshape | solution.py:216
  20.5 0.0 copy-start.2
  20.5 45.5 %nest_block.1 = (bf16[8,2,64,16,128]{4,3,2,1,0:T(8,128)(2,1)}, bf16[2048,512]{1,0:T(8,128)(2,1)}, bf16[256,512]{1,0:T(8,128)(2,1)}) custom-call(bf16[2048,512]{1,0:T(8,128)(2,1)} %fusion.refs_0_, bf16[2048,512]{1,0:T(8,128)(2,1)} %select_bitcast_fusion.refs_1_, bf16[512,2048]{1,0:T(8,128)(2,1)} %refs_2_.1, bf16[2048,512]{1,0:T(8,128)(2,1)} %refs_3_.1), custom_call_target="tpu_custom_call" | custom-call | tf_op jit(solution)/shard_map/nest_block/pallas_call | solution.py:221
  66.0 0.0 copy-done.2
  66.0 1.4 %fusion.4 = f32[512,512]{1,0:T(8,128)S(1)} fusion(bf16[256,512]{1,0:T(8,128)(2,1)} %get-tuple-element.9, s32[256]{0:T(256)S(1)} %copy-done.2, pred[256]{0:T(512)(128)(4,1)S(1)} %iota_compare_fusion.1), kind=kOutput, calls=%fused_computation.17 | convolution fusion | flops 134479872 | bytes 1312000 | tf_op jit(solution)/shard_map/dot_general | solution.py:236
  67.4 3.1 %bitcast_select_fusion = bf16[256,8,512]{2,1,0:T(8,128)(2,1)} fusion(bf16[2048,512]{1,0:T(8,128)(2,1)} %get-tuple-element.10, pred[256]{0:T(512)(128)(4,1)S(1)} %iota_compare_fusion.1), kind=kLoop, calls=%fused_computation.3 | loop fusion | flops 1048576 | bytes 4194560 | tf_op jit(solution)/shard_map/jit(_where)/select_n | solution.py:234
  70.5 1.0 add_convert_fusion.1
  71.5 47.7 %reduce_all.1 = (bf16[512,2048]{1,0:T(8,128)(2,1)}, bf16[2048,512]{1,0:T(8,128)(2,1)}) custom-call(bf16[8,2,64,16,128]{4,3,2,1,0:T(8,128)(2,1)} %get-tuple-element.11.part), custom_call_target="tpu_custom_call" | custom-call | tf_op jit(solution)/shard_map/reduce_all/pallas_call | solution.py:238
  119.2 0.0 copy-start.1
  119.2 4.3 %convert_element_type.31 = f32[512,2048]{1,0:T(8,128)} convert(bf16[512,2048]{1,0:T(8,128)(2,1)} %get-tuple-element.12) | non-fusion elementwise | flops 1048576 | bytes 6291456 | tf_op jit(solution)/shard_map/convert_element_type | solution.py:256
  123.5 0.0 copy-done.1
  123.5 2.6 %convert_element_type.32 = f32[2048,512]{1,0:T(8,128)} convert(bf16[2048,512]{1,0:T(8,128)(2,1)S(1)} %copy-done.1) | non-fusion elementwise | flops 1048576 | bytes 6291456 | tf_op jit(solution)/shard_map/convert_element_type | solution.py:256
  (2 shorter events, 0.0 us)
Async XLA Ops:
  1.4 13.9 %collective-permute-start = (bf16[1,32,512]{2,1,0:T(8,128)(2,1)S(1)}, bf16[1,32,512]{2,1,0:T(8,128)(2,1)S(1)}, u32[]{:S(2)}, u32[]{:S(2)}) collective-permute-start(bf16[1,32,512]{2,1,0:T(8,128)(2,1)S(1)} %get-tuple-element.14), channel_id=1, source_target_pairs={{0,8},{8,16},{16,24},{24,32},{32,40},{40,48},{48,56},{56,64},{64,7... | collective-permute-start | bytes 98312 | tf_op jit(solution)/shard_map/ppermute | solution.py:30
  5.3 10.0 %collective-permute-start.1 = (bf16[1,32,512]{2,1,0:T(8,128)(2,1)S(1)}, bf16[1,32,512]{2,1,0:T(8,128)(2,1)S(1)}, u32[]{:S(2)}, u32[]{:S(2)}) collective-permute-start(bf16[1,32,512]{2,1,0:T(8,128)(2,1)S(1)} %get-tuple-element.15), channel_id=1, source_target_pairs={{8,0},{16,8},{24,16},{32,24},{40,32},{48,40},{56,48},{64,56},{72,6... | collective-permute-start | bytes 98312 | tf_op jit(solution)/shard_map/ppermute | solution.py:31
  7.7 7.4 %collective-permute-start.2 = (bf16[16,1,512]{2,1,0:T(2,128)(2,1)S(1)}, bf16[16,1,512]{2,1,0:T(2,128)(2,1)S(1)}, u32[]{:S(2)}, u32[]{:S(2)}) collective-permute-start(bf16[16,1,512]{2,1,0:T(2,128)(2,1)S(1)} %get-tuple-element.16), channel_id=1, source_target_pairs={{0,1},{1,2},{2,3},{3,4},{4,5},{5,6},{6,7},{7,0},{8,9},{9,10},{10,1... | collective-permute-start | bytes 49160 | tf_op jit(solution)/shard_map/ppermute | solution.py:30
  9.8 5.2 %collective-permute-start.3 = (bf16[16,1,512]{2,1,0:T(2,128)(2,1)S(1)}, bf16[16,1,512]{2,1,0:T(2,128)(2,1)S(1)}, u32[]{:S(2)}, u32[]{:S(2)}) collective-permute-start(bf16[16,1,512]{2,1,0:T(2,128)(2,1)S(1)} %get-tuple-element.17), channel_id=1, source_target_pairs={{1,0},{2,1},{3,2},{4,3},{5,4},{6,5},{7,6},{0,7},{9,8},{10,9},{11,1... | collective-permute-start | bytes 49160 | tf_op jit(solution)/shard_map/ppermute | solution.py:31
  11.9 3.2 %copy-start = (bf16[16,32,512]{2,1,0:T(8,128)(2,1)S(1)}, bf16[16,32,512]{2,1,0:T(8,128)(2,1)}, u32[]{:S(2)}) copy-start(bf16[16,32,512]{2,1,0:T(8,128)(2,1)} %param.8) | copy-start | bytes 1572868
  15.0 0.7 copy-start.3
  20.5 45.5 %copy-start.2 = (s32[256]{0:T(256)S(1)}, s32[256]{0:T(256)}, u32[]{:S(2)}) copy-start(s32[256]{0:T(256)} %param.13) | copy-start | bytes 3076
  119.2 4.3 %copy-start.1 = (bf16[2048,512]{1,0:T(8,128)(2,1)S(1)}, bf16[2048,512]{1,0:T(8,128)(2,1)}, u32[]{:S(2)}) copy-start(bf16[2048,512]{1,0:T(8,128)(2,1)} %get-tuple-element.13) | copy-start | bytes 6291460

commit v2 on v1

v2 whole, which is shorter than its diff:
```python
import math

import jax
import jax.numpy as jnp
from jax import lax
from jax.experimental import pallas as pl
from jax.experimental.pallas import tpu as pltpu
from jax.sharding import PartitionSpec as P

MESH = pl.DeviceIdType.MESH
F32 = jnp.float32
BF16 = jnp.bfloat16
NT = (((1,), (1,)), ((), ()))
TN = (((0,), (0,)), ((), ()))
G0 = math.sqrt(2.0 / math.pi)
G1 = G0 * 0.044715
CH = 256
NCH = 8
VMEM = pl.BlockSpec(memory_space=pltpu.VMEM)
PLANE = [(a, b) for a in range(4) for b in range(4) if a or b]


def gelu_pair(h, da):
    h2 = h * h
    s = 0.5 + 0.5 * jnp.tanh(h * (G0 + G1 * h2))
    act = h * s
    slope = s + act * (1.0 - s) * (2.0 * G0 + 6.0 * G1 * h2)
    return act.astype(BF16), (slope * da).astype(BF16)


class Place:
    def __init__(self):
        a, b = lax.axis_index("lat"), lax.axis_index("lon")
        self.x, self.y, self.z = lax.rem(a, 4), b // 2, a // 4
        self.core = lax.rem(b, 2)

    def to(self, dx, dy, dz):
        x, y, z = lax.rem(self.x + dx, 4), lax.rem(self.y + dy, 4), lax.rem(self.z + dz, 4)
        return (z * 4 + x, y * 2 + self.core)

    def partner(self):
        return (self.z * 4 + self.x, self.y * 2 + 1 - self.core)

    def side(self):
        return (self.z * 4 + self.x, lax.rem(self.y + 2 * self.core + 3, 4) * 2 + 1 - self.core)

    def lat(self, d):
        return (lax.rem(self.z * 4 + self.x + d, 16), self.y * 2 + self.core)

    def lon(self, d):
        return (self.z * 4 + self.x, lax.rem(self.y * 2 + self.core + d, 8))

    def axis(self, a):
        ex, ez = (2 - a) // 2, a // 2
        ey = 1 - ex - ez
        return ((ex, ey, ez), self.x * ex + self.y * ey + self.z * ez)


class Reduce:
    def __init__(self, part, full, rc, half, ra, qb, rp, send, recv):
        self.part, self.full, self.rc, self.half = part, full, rc, half
        self.ra, self.qb, self.rp, self.send, self.recv = ra, qb, rp, send, recv
        self.at = Place()

    def sets(self, c):
        a0 = lax.rem(c, 3)
        (e0, q) = self.at.axis(a0)
        (e1, u) = self.at.axis(lax.rem(a0 + 1, 3))
        (e2, v) = self.at.axis(lax.rem(a0 + 2, 3))
        return e0, e1, e2, q, u, v

    def copy(self, src, dst, stage, c, device):
        pltpu.make_async_remote_copy(
            src_ref=src, dst_ref=dst, send_sem=self.send.at[stage, c], recv_sem=self.recv.at[stage, c],
            device_id=device, device_id_type=MESH,
        ).start()

    def wait(self, ref, stage, c):
        pltpu.make_async_copy(ref, ref, self.recv.at[stage, c]).wait()

    def greet(self):
        barrier = pltpu.get_barrier_semaphore()
        others = [self.at.partner(), self.at.side()]
        for dx in range(4):
            for dy in range(4):
                for dz in range(4):
                    if (dx or dy or dz) and not (dx and dy and dz):
                        others.append(self.at.to(dx, dy, dz))
        for device in others:
            pl.semaphore_signal(barrier, inc=1, device_id=device, device_id_type=MESH)
        return barrier, len(others)

    def s0(self, c):
        self.copy(self.part.at[c, 1 - self.at.core], self.rc.at[c], 0, c, self.at.partner())

    def s1(self, c):
        e0, e1, e2, q, u, v = self.sets(c)
        self.wait(self.rc.at[c], 0, c)
        self.half[c] = (self.part[c, self.at.core].astype(F32) + self.rc[c].astype(F32)).astype(BF16)
        for d in (1, 2, 3):
            to = lax.rem(q + d, 4)
            self.copy(self.half.at[c, pl.ds(to * 16, 16)], self.ra.at[c, d - 1], 1, c, self.at.to(*(d * e for e in e0)))

    def s2(self, c):
        e0, e1, e2, q, u, v = self.sets(c)
        self.wait(self.ra.at[c], 1, c)
        mine = pl.ds(q * 16, 16)
        total = self.part[c, self.at.core, mine].astype(F32) + self.rc[c, mine].astype(F32)
        for d in range(3):
            total += self.ra[c, d].astype(F32)
        self.qb[c] = total.astype(BF16)
        for o, (d1, d2) in enumerate(PLANE):
            to = lax.rem(u + d1, 4) * 4 + lax.rem(v + d2, 4)
            self.copy(self.qb.at[c, to], self.rp.at[c, o], 2, c, self.at.to(*(d1 * f + d2 * g for f, g in zip(e1, e2))))

    def s3(self, c):
        e0, e1, e2, q, u, v = self.sets(c)
        self.wait(self.rp.at[c], 2, c)
        total = self.qb[c, u * 4 + v].astype(F32)
        for o in range(15):
            total += self.rp[c, o].astype(F32)
        spot = self.full.at[c, self.at.core, q * 16 + u * 4 + v]
        spot[...] = total.astype(BF16)
        for d1, d2 in PLANE:
            self.copy(spot, spot, 3, c, self.at.to(*(d1 * f + d2 * g for f, g in zip(e1, e2))))

    def s4(self, c):
        e0, e1, e2, q, u, v = self.sets(c)
        self.wait(self.rp.at[c], 3, c)
        spot = self.full.at[c, self.at.core, pl.ds(q * 16, 16)]
        for d in (1, 2, 3):
            self.copy(spot, spot, 4, c, self.at.to(*(d * e for e in e0)))

    def s5(self, c):
        self.wait(self.ra.at[c], 4, c)
        spot = self.full.at[c, self.at.core]
        self.copy(spot, spot, 5, c, self.at.partner())

    def s6(self, c, gi, go):
        self.wait(self.full.at[c, 1 - self.at.core], 5, c)
        for k in range(2):
            cols = pl.ds(pl.multiple_of(c * CH + 128 * k, 128), 128)
            gi[:, cols] = self.full[c, 0, 32 * k : 32 * k + 32].reshape(512, 128)
        for k in range(4):
            rows = pl.ds(pl.multiple_of(c * CH, CH), CH)
            go[rows, 128 * k : 128 * k + 128] = self.full[c, 1, 16 * k : 16 * k + 16].reshape(256, 128)

    def drain(self, c):
        for stage, ref in enumerate((self.rc, self.ra, self.rp, self.rp, self.ra, self.rc)):
            pltpu.make_async_copy(ref.at[c], ref.at[c], self.send.at[stage, c]).wait()


def every(n, fn):
    def body(i, carry):
        fn(i)
        return carry

    lax.fori_loop(0, n, body, 0)


def rows_of(r, n):
    return pl.ds(pl.multiple_of(r * n, n), n)


def step_kernel(
    factor, count, parent_h, diff, nest_h, cot_h, pos, wi_h, wo_h,
    pout, dx, gi, go,
    ext, edge, beside, sm, x, xT, cot, wi, wo, da, act, dh, fb, load, hs, hr, part, *scratch,
):
    r = Reduce(part, *scratch)
    at = r.at
    loads = [
        pltpu.make_async_copy(src, dst, load.at[i])
        for i, (src, dst) in enumerate(((parent_h, ext.at[pl.ds(1, 16)]), (cot_h, cot), (wo_h, wo), (nest_h, x), (wi_h, wi)))
    ]
    for c in loads:
        c.start()
    barrier, met = r.greet()
    live = count[0]

    loads[0].wait()
    for i in range(16):
        line = ext[1 + i].astype(F32)
        edge[0, i : i + 1] = line[0:1]
        edge[1, i : i + 1] = line[31:32]
    loads[1].wait()

    def mask(t):
        rows = rows_of(t, 256)
        index = lax.broadcasted_iota(jnp.int32, (256, 512), 0) + t * 256
        cot[rows, :] = jnp.where(index < live * 8, cot[rows, :].astype(F32), 0.0).astype(BF16)

    every(8, mask)
    pl.semaphore_wait(barrier, met)

    def halo(i, src, dst, device):
        c = pltpu.make_async_remote_copy(
            src_ref=src, dst_ref=dst, send_sem=hs.at[i], recv_sem=hr.at[i], device_id=device, device_id_type=MESH
        )
        c.start()
        return c

    halos = [
        halo(0, ext.at[16], ext.at[0], at.lat(1)),
        halo(1, ext.at[1], ext.at[17], at.lat(15)),
        halo(2, edge.at[1], beside.at[0], at.lon(1)),
        halo(3, edge.at[0], beside.at[1], at.lon(7)),
    ]
    loads[2].wait()

    def first_da(t):
        rows = rows_of(t, 512)
        da[rows, :] = lax.dot_general(cot[rows, :], wo[pl.ds(0, CH), :], NT, preferred_element_type=F32)

    every(4, first_da)
    cells = lax.broadcasted_iota(jnp.int32, (512, 256), 0)
    slots = lax.broadcasted_iota(jnp.int32, (512, 256), 1)
    hot = jnp.where((cells == pos[...]) & (slots < live), 1.0, 0.0).astype(BF16)
    for c in halos:
        c.wait()

    band = lax.axis_index("lat")

    @pl.when(band == 0)
    def _():
        ext[0] = jnp.zeros_like(ext[0])

    @pl.when(band == 15)
    def _():
        ext[17] = jnp.zeros_like(ext[17])

    west, east = beside[0], beside[1]
    column = lax.broadcasted_iota(jnp.int32, (32, 512), 0)
    rate = diff[...]
    for i in range(16):
        f = ext[1 + i].astype(F32)
        w = jnp.where(column == 0, west[i : i + 1], pltpu.roll(f, 1, 0))
        e = jnp.where(column == 31, east[i : i + 1], pltpu.roll(f, 31, 0))
        near = ext[i].astype(F32) + ext[2 + i].astype(F32) + w + e - 4.0 * f
        sm[32 * i : 32 * i + 32] = f + rate * near
    field = sm[...]
    high = field.astype(BF16)
    low = (field - high.astype(F32)).astype(BF16)
    context = lax.dot_general(hot, high, TN, preferred_element_type=F32)
    context += lax.dot_general(hot, low, TN, preferred_element_type=F32)
    loads[3].wait()
    for t in range(4):
        rows = pl.ds(t * 512, 512)
        wide = jnp.broadcast_to(context[64 * t : 64 * t + 64, None, :], (64, 8, 512)).reshape(512, 512)
        x[rows, :] = (x[rows, :].astype(F32) + wide).astype(BF16)
    loads[4].wait()
    xT[...] = x[...].T

    def tiles(j, first):
        cols = rows_of(j, CH)

        def tile(t):
            rows = rows_of(t, 512)
            h = jnp.dot(x[rows, :], wi[:, cols], preferred_element_type=F32)
            if first:
                d = da[rows, :]
            else:
                d = lax.dot_general(cot[rows, :], wo[cols, :], NT, preferred_element_type=F32)
            a, d = gelu_pair(h, d)
            act[rows, cols] = a
            dh[rows, cols] = d

        every(4, tile)

    def grads(j):
        cols = rows_of(j, CH)
        g = jnp.dot(xT[...], dh[:, cols], preferred_element_type=F32) * factor
        for k in range(2):
            part[j, 0, 32 * k : 32 * k + 32] = g[:, 128 * k : 128 * k + 128].astype(BF16).reshape(32, 16, 128)
        g = lax.dot_general(act[:, cols], cot[...], TN, preferred_element_type=F32) * factor
        for k in range(4):
            part[j, 1, 16 * k : 16 * k + 16] = g[:, 128 * k : 128 * k + 128].astype(BF16).reshape(16, 16, 128)

    def rest(t):
        rows = rows_of(t, 256)
        d = lax.dot_general(dh[rows, :], wi[...], NT, preferred_element_type=F32)
        dx[rows, :] = (d + cot[rows, :].astype(F32)).astype(BF16)
        o = jnp.dot(act[rows, :], wo[...], preferred_element_type=F32) + x[rows, :].astype(F32)
        fb[rows_of(t, 32), :] = jnp.mean(o.reshape(32, 8, 512), axis=1).astype(BF16)

    def stages(s, *pairs):
        for stage, delay in pairs:
            c = s - delay

            @pl.when((c >= 0) & (c < NCH))
            def _():
                stage(c)

    odd = ((r.s1, 1), (r.s3, 4), (r.s5, 7))
    even = ((r.s2, 2), (r.s4, 5), (lambda c: r.s6(c, gi, go), 7))
    tiles(0, True)

    def slot(s):
        @pl.when(s > 0)
        def _():
            tiles(s, False)

        stages(s, *odd)
        grads(s)
        r.s0(s)
        stages(s, *even)

    every(NCH, slot)

    def late(i):
        @pl.when(i < 4)
        def _():
            rest(2 * i)

        stages(i + 8, *odd)

        @pl.when(i < 4)
        def _():
            rest(2 * i + 1)

        @pl.when(i == 4)
        def _():
            pout[...] = (sm[...] + jnp.dot(hot, fb[...], preferred_element_type=F32)).astype(BF16)

        stages(i + 8, *even)

    every(7, late)
    every(NCH, r.drain)


def local(parent, diffusion, nest_state, nest_cotangent, owner_count, tile_pos, w_in, w_out):
    blat, blon, chans = parent.shape
    own_tiles, tile_rows = (nest_state.shape[0], nest_state.shape[1])
    rows, cells, hidden = own_tiles * tile_rows, blat * blon, w_in.shape[1]
    devices = lax.axis_size(("lat", "lon"))
    factor = 1.0 / math.sqrt(own_tiles * devices // 4 * tile_rows)
    hbm = pl.BlockSpec(memory_space=pl.ANY)
    parent_out, nest_grad, grad_in, grad_out = pl.pallas_call(
        lambda *refs: step_kernel(factor, *refs),
        out_shape=[
            jax.ShapeDtypeStruct((cells, chans), BF16),
            jax.ShapeDtypeStruct((rows, chans), BF16),
            jax.ShapeDtypeStruct(w_in.shape, BF16),
            jax.ShapeDtypeStruct(w_out.shape, BF16),
        ],
        in_specs=[pl.BlockSpec(memory_space=pltpu.SMEM), hbm, VMEM, hbm, hbm, VMEM, hbm, hbm],
        out_specs=[VMEM] * 4,
        scratch_shapes=[
            pltpu.VMEM((blat + 2, blon, chans), BF16),
            pltpu.VMEM((2, blat, chans), F32),
            pltpu.VMEM((2, blat, chans), F32),
            pltpu.VMEM((cells, chans), F32),
            pltpu.VMEM((rows, chans), BF16),
            pltpu.VMEM((chans, rows), BF16),
            pltpu.VMEM((rows, chans), BF16),
            pltpu.VMEM(w_in.shape, BF16),
            pltpu.VMEM(w_out.shape, BF16),
            pltpu.VMEM((rows, CH), F32),
            pltpu.VMEM((rows, hidden), BF16),
            pltpu.VMEM((rows, hidden), BF16),
            pltpu.VMEM((own_tiles, chans), BF16),
            pltpu.SemaphoreType.DMA((5,)),
            pltpu.SemaphoreType.DMA((4,)),
            pltpu.SemaphoreType.DMA((4,)),
            pltpu.VMEM((NCH, 2, 64, 16, 128), BF16),
            pltpu.VMEM((NCH, 2, 64, 16, 128), BF16),
            pltpu.VMEM((NCH, 64, 16, 128), BF16),
            pltpu.VMEM((NCH, 64, 16, 128), BF16),
            pltpu.VMEM((NCH, 3, 16, 16, 128), BF16),
            pltpu.VMEM((NCH, 16, 16, 128), BF16),
            pltpu.VMEM((NCH, 15, 16, 128), BF16),
            pltpu.SemaphoreType.DMA((6, NCH)),
            pltpu.SemaphoreType.DMA((6, NCH)),
        ],
        compiler_params=pltpu.CompilerParams(collective_id=0, has_side_effects=True, vmem_limit_bytes=60 * 2**20),
        name="nest_step",
    )(
        owner_count, parent, diffusion.reshape(1, chans), nest_state.reshape(rows, chans),
        nest_cotangent.reshape(rows, chans), tile_pos.reshape(1, own_tiles), w_in, w_out,
    )
    return (
        parent_out.reshape(parent.shape), nest_grad.reshape(nest_state.shape),
        grad_in.astype(F32), grad_out.astype(F32),
    )


def solution(mesh):
    in_specs = (
        P("lat", "lon", None),
        P(),
        P(("lat", "lon"), None, None),
        P(("lat", "lon"), None, None),
        P(("lat", "lon")),
        P(("lat", "lon")),
        P(),
        P(),
    )
    out_specs = (P("lat", "lon", None), P(("lat", "lon"), None, None), P(), P())
    return jax.shard_map(local, mesh=mesh, in_specs=in_specs, out_specs=out_specs, check_vma=False)
```

time: 127 us -> 86.6 us (0.68)
  Pallas kernels: 93.2 us -> 76.2 us
  other arithmetic: 19.6 us -> 6.89 us
  starting transfers between devices: 7.37 us -> 0 us
  matrix products: 1.4 us -> 0 us
    pallas_call x2 -> x1, Pallas kernels: 93.2 us -> 76.2 us  [local(): pl.pallas_call(lambda *refs: step_kernel(factor, *refs), out_shape=[jax.S...]
    ppermute x4 -> x0, starting transfers between devices: 7.37 us -> none  [the longest x2 6.07 us: extended(): before = lax.ppermute(last, axis, up)]
    reshape x2 -> x0, other arithmetic: 6.5 us -> none  [the longest x1 3.34 us: local(): (nest_state.astype(F32) + context[:, None, :]).astype(BF16)]
    select_n x3 -> x0, other arithmetic: 3.89 us -> none  [the longest x1 3.1 us: local(): jnp.where(live[:, None, None], d_inputs.reshape(nest_state.shape), jnp.ze...]
    unnamed x8, local copies, waits for them, and re-layouts: 0.28 us -> 2.12 us
    slice x2 -> x0, local copies, waits for them, and re-layouts: 1.81 us -> none  [extended(): last = lax.slice_in_dim(x, length - width, length, axis=dim)]
    dot_general x1 -> x0, matrix products: 1.4 us -> none  [local(): summed = jnp.dot(onehot.T, feedback, preferred_element_type=F32)]
    convert_element_type x5 -> x2, other arithmetic: 8.19 us -> 6.89 us  [the longest x1 4.28 us: local(): grad_in.astype(F32)]
  transfers between devices with their start and end apart: 4 -> 0, of which waited for: 0 -> 0; matrix products, arithmetic and copies ran while one was open for 5% -> 0% of each run, Pallas kernels for 0% -> 0%
where the time goes in v2:
time: 86.6 us; the launch traced here: 86.5 us
  Pallas kernels  76.2 us (88%)
  other arithmetic  6.89 us (8%)
  local copies, waits for them, and re-layouts  2.12 us (2%)
  between operations  1.3 us (2%)
    pallas_call x1, Pallas kernels, local(): pl.pallas_call(lambda *refs: step_kernel(factor, *refs), out_shape=[jax.S...  76.2 us
    convert_element_type x1, other arithmetic, local(): grad_in.astype(F32)  4.28 us
    convert_element_type x1, other arithmetic, local(): grad_out.astype(F32)  2.61 us
    unnamed x8, local copies, waits for them, and re-layouts  2.12 us

profile of v2, /device:TPU:1, one launch (start us, length us, event | category | flops | bytes accessed | tf_op | source)
XLA Modules:
  0.0 86.5 jit_solution(6291082505522279237)
XLA Ops:
  1.3 76.2 %nest_step.1 = (bf16[512,512]{1,0:T(8,128)(2,1)}, bf16[2048,512]{1,0:T(8,128)(2,1)}, bf16[512,2048]{1,0:T(8,128)(2,1)}, bf16[2048,512]{1,0:T(8,128)(2,1)}) custom-call(s32[1]{0:T(128)S(6)} %copy.14.refs_0_, bf16[16,32,512]{2,1,0:T(8,128)(2,1)} %refs_1_.1, f32[1,512]{1,0:T(1,128)} %bitcast.10, bf16[2048,512]{1,0:T(8,128)(2,1)} %bitcast.7, ...), custom_call_target="tpu_custom_call" | custom-call | tf_op jit(solution)/shard_map/nest_step/pallas_call | solution.py:338
  77.5 0.0 copy-start
  77.5 4.3 %convert_element_type.6 = f32[512,2048]{1,0:T(8,128)} convert(bf16[512,2048]{1,0:T(8,128)(2,1)} %get-tuple-element.10) | non-fusion elementwise | flops 1048576 | bytes 6291456 | tf_op jit(solution)/shard_map/convert_element_type | solution.py:383
  81.8 0.0 copy-done
  81.8 0.0 copy-start.2
  81.8 0.0 copy-start.1
  81.8 2.6 %convert_element_type.7 = f32[2048,512]{1,0:T(8,128)} convert(bf16[2048,512]{1,0:T(8,128)(2,1)S(1)} %copy-done) | non-fusion elementwise | flops 1048576 | bytes 6291456 | tf_op jit(solution)/shard_map/convert_element_type | solution.py:383
  84.4 0.0 copy-done.2
  84.4 0.8 copy.15
  85.2 0.0 copy-done.1
  85.2 1.3 %copy.16 = bf16[256,8,512]{2,1,0:T(8,128)(2,1)} copy(bf16[256,8,512]{2,1,0:T(8,128)(2,1)S(1)} %bitcast.6) | data formatting | bytes 4194304
Async XLA Ops:
  77.5 4.3 %copy-start = (bf16[2048,512]{1,0:T(8,128)(2,1)S(1)}, bf16[2048,512]{1,0:T(8,128)(2,1)}, u32[]{:S(2)}) copy-start(bf16[2048,512]{1,0:T(8,128)(2,1)} %get-tuple-element.11) | copy-start | bytes 6291460
  81.8 2.6 %copy-start.2 = (bf16[512,512]{1,0:T(8,128)(2,1)S(1)}, bf16[512,512]{1,0:T(8,128)(2,1)}, u32[]{:S(2)}) copy-start(bf16[512,512]{1,0:T(8,128)(2,1)} %get-tuple-element.8) | copy-start | bytes 1572868
  81.8 3.4 %copy-start.1 = (bf16[2048,512]{1,0:T(8,128)(2,1)S(1)}, bf16[2048,512]{1,0:T(8,128)(2,1)}, u32[]{:S(2)}) copy-start(bf16[2048,512]{1,0:T(8,128)(2,1)} %get-tuple-element.9) | copy-start | bytes 6291460

commit v3 on v2

--- a/solution.py
+++ b/solution.py
@@ -136,14 +136,9 @@
         spot = self.full.at[c, self.at.core]
         self.copy(spot, spot, 5, c, self.at.partner())
 
-    def s6(self, c, gi, go):
+    def s6(self, c, sums, out):
         self.wait(self.full.at[c, 1 - self.at.core], 5, c)
-        for k in range(2):
-            cols = pl.ds(pl.multiple_of(c * CH + 128 * k, 128), 128)
-            gi[:, cols] = self.full[c, 0, 32 * k : 32 * k + 32].reshape(512, 128)
-        for k in range(4):
-            rows = pl.ds(pl.multiple_of(c * CH, CH), CH)
-            go[rows, 128 * k : 128 * k + 128] = self.full[c, 1, 16 * k : 16 * k + 16].reshape(256, 128)
+        pltpu.make_async_copy(self.full.at[c], sums.at[c], out.at[c]).start()
 
     def drain(self, c):
         for stage, ref in enumerate((self.rc, self.ra, self.rp, self.rp, self.ra, self.rc)):
@@ -164,8 +159,8 @@
 
 def step_kernel(
     factor, count, parent_h, diff, nest_h, cot_h, pos, wi_h, wo_h,
-    pout, dx, gi, go,
-    ext, edge, beside, sm, x, xT, cot, wi, wo, da, act, dh, fb, load, hs, hr, part, *scratch,
+    pout, dx, sums,
+    ext, edge, beside, sm, x, xT, cot, wi, wo, da, act, dh, fb, field_out, load, out, hs, hr, part, *scratch,
 ):
     r = Reduce(part, *scratch)
     at = r.at
@@ -173,7 +168,7 @@
         pltpu.make_async_copy(src, dst, load.at[i])
         for i, (src, dst) in enumerate(((parent_h, ext.at[pl.ds(1, 16)]), (cot_h, cot), (wo_h, wo), (nest_h, x), (wi_h, wi)))
     ]
-    for c in loads:
+    for c in loads[:3]:
         c.start()
     barrier, met = r.greet()
     live = count[0]
@@ -183,14 +178,6 @@
         line = ext[1 + i].astype(F32)
         edge[0, i : i + 1] = line[0:1]
         edge[1, i : i + 1] = line[31:32]
-    loads[1].wait()
-
-    def mask(t):
-        rows = rows_of(t, 256)
-        index = lax.broadcasted_iota(jnp.int32, (256, 512), 0) + t * 256
-        cot[rows, :] = jnp.where(index < live * 8, cot[rows, :].astype(F32), 0.0).astype(BF16)
-
-    every(8, mask)
     pl.semaphore_wait(barrier, met)
 
     def halo(i, src, dst, device):
@@ -206,13 +193,18 @@
         halo(2, edge.at[1], beside.at[0], at.lon(1)),
         halo(3, edge.at[0], beside.at[1], at.lon(7)),
     ]
+    for c in loads[3:]:
+        c.start()
+
+    def mask(t):
+        rows = rows_of(t, 256)
+        index = lax.broadcasted_iota(jnp.int32, (256, 512), 0) + t * 256
+        cot[rows, :] = jnp.where(index < live * 8, cot[rows, :].astype(F32), 0.0).astype(BF16)
+
+    loads[1].wait()
+    every(8, mask)
     loads[2].wait()
-
-    def first_da(t):
-        rows = rows_of(t, 512)
-        da[rows, :] = lax.dot_general(cot[rows, :], wo[pl.ds(0, CH), :], NT, preferred_element_type=F32)
-
-    every(4, first_da)
+    da[...] = lax.dot_general(cot[...], wo[pl.ds(0, CH), :], NT, preferred_element_type=F32)
     cells = lax.broadcasted_iota(jnp.int32, (512, 256), 0)
     slots = lax.broadcasted_iota(jnp.int32, (512, 256), 1)
     hot = jnp.where((cells == pos[...]) & (slots < live), 1.0, 0.0).astype(BF16)
@@ -254,18 +246,11 @@
     def tiles(j, first):
         cols = rows_of(j, CH)
 
-        def tile(t):
-            rows = rows_of(t, 512)
-            h = jnp.dot(x[rows, :], wi[:, cols], preferred_element_type=F32)
-            if first:
-                d = da[rows, :]
-            else:
-                d = lax.dot_general(cot[rows, :], wo[cols, :], NT, preferred_element_type=F32)
-            a, d = gelu_pair(h, d)
-            act[rows, cols] = a
-            dh[rows, cols] = d
-
-        every(4, tile)
+        h = jnp.dot(x[...], wi[:, cols], preferred_element_type=F32)
+        d = da[...] if first else lax.dot_general(cot[...], wo[cols, :], NT, preferred_element_type=F32)
+        a, d = gelu_pair(h, d)
+        act[:, cols] = a
+        dh[:, cols] = d
 
     def grads(j):
         cols = rows_of(j, CH)
@@ -279,7 +264,8 @@
     def rest(t):
         rows = rows_of(t, 256)
         d = lax.dot_general(dh[rows, :], wi[...], NT, preferred_element_type=F32)
-        dx[rows, :] = (d + cot[rows, :].astype(F32)).astype(BF16)
+        cot[rows, :] = (d + cot[rows, :].astype(F32)).astype(BF16)
+        pltpu.make_async_copy(cot.at[rows], dx.at[rows], out.at[t]).start()
         o = jnp.dot(act[rows, :], wo[...], preferred_element_type=F32) + x[rows, :].astype(F32)
         fb[rows_of(t, 32), :] = jnp.mean(o.reshape(32, 8, 512), axis=1).astype(BF16)
 
@@ -291,8 +277,8 @@
             def _():
                 stage(c)
 
-    odd = ((r.s1, 1), (r.s3, 4), (r.s5, 7))
-    even = ((r.s2, 2), (r.s4, 5), (lambda c: r.s6(c, gi, go), 7))
+    odd = ((r.s1, 1), (r.s3, 4), (r.s5, 7),)
+    even = ((r.s2, 2), (r.s4, 5), ((lambda c: r.s6(c, sums, out.at[pl.ds(8, NCH)])), 7),)
     tiles(0, True)
 
     def slot(s):
@@ -320,12 +306,30 @@
 
         @pl.when(i == 4)
         def _():
-            pout[...] = (sm[...] + jnp.dot(hot, fb[...], preferred_element_type=F32)).astype(BF16)
+            field_out[...] = (sm[...] + jnp.dot(hot, fb[...], preferred_element_type=F32)).astype(BF16)
+            pltpu.make_async_copy(field_out, pout, out.at[16]).start()
 
         stages(i + 8, *even)
 
     every(7, late)
     every(NCH, r.drain)
+
+    def leave(t):
+        rows = rows_of(t, 256)
+        pltpu.make_async_copy(cot.at[rows], dx.at[rows], out.at[t]).wait()
+        pltpu.make_async_copy(r.full.at[t], sums.at[t], out.at[8 + t]).wait()
+
+    every(8, leave)
+    pltpu.make_async_copy(field_out, pout, out.at[16]).wait()
+
+
+def finish_kernel(sums, dx_in, field_in, gi, go, dx, field):
+    for k in range(2):
+        gi[:, 128 * k : 128 * k + 128] = sums[0, 0, 32 * k : 32 * k + 32].reshape(512, 128).astype(F32)
+    for k in range(4):
+        go[:, 128 * k : 128 * k + 128] = sums[0, 1, 16 * k : 16 * k + 16].reshape(256, 128).astype(F32)
+    dx[...] = dx_in[...]
+    field[...] = field_in[...]
 
 
 def local(parent, diffusion, nest_state, nest_cotangent, owner_count, tile_pos, w_in, w_out):
@@ -335,16 +339,15 @@
     devices = lax.axis_size(("lat", "lon"))
     factor = 1.0 / math.sqrt(own_tiles * devices // 4 * tile_rows)
     hbm = pl.BlockSpec(memory_space=pl.ANY)
-    parent_out, nest_grad, grad_in, grad_out = pl.pallas_call(
+    parent_out, nest_grad, sums = pl.pallas_call(
         lambda *refs: step_kernel(factor, *refs),
         out_shape=[
             jax.ShapeDtypeStruct((cells, chans), BF16),
             jax.ShapeDtypeStruct((rows, chans), BF16),
-            jax.ShapeDtypeStruct(w_in.shape, BF16),
-            jax.ShapeDtypeStruct(w_out.shape, BF16),
+            jax.ShapeDtypeStruct((NCH, 2, 64, 16, 128), BF16),
         ],
         in_specs=[pl.BlockSpec(memory_space=pltpu.SMEM), hbm, VMEM, hbm, hbm, VMEM, hbm, hbm],
-        out_specs=[VMEM] * 4,
+        out_specs=[hbm] * 3,
         scratch_shapes=[
             pltpu.VMEM((blat + 2, blon, chans), BF16),
             pltpu.VMEM((2, blat, chans), F32),
@@ -359,7 +362,9 @@
             pltpu.VMEM((rows, hidden), BF16),
             pltpu.VMEM((rows, hidden), BF16),
             pltpu.VMEM((own_tiles, chans), BF16),
+            pltpu.VMEM((cells, chans), BF16),
             pltpu.SemaphoreType.DMA((5,)),
+            pltpu.SemaphoreType.DMA((17,)),
             pltpu.SemaphoreType.DMA((4,)),
             pltpu.SemaphoreType.DMA((4,)),
             pltpu.VMEM((NCH, 2, 64, 16, 128), BF16),
@@ -378,10 +383,22 @@
         owner_count, parent, diffusion.reshape(1, chans), nest_state.reshape(rows, chans),
         nest_cotangent.reshape(rows, chans), tile_pos.reshape(1, own_tiles), w_in, w_out,
     )
-    return (
-        parent_out.reshape(parent.shape), nest_grad.reshape(nest_state.shape),
-        grad_in.astype(F32), grad_out.astype(F32),
-    )
+    slab = lambda n: pl.BlockSpec((n, chans), lambda i: (i, 0))
+    grad_in, grad_out, nest_grad, parent_out = pl.pallas_call(
+        finish_kernel,
+        grid=(NCH,),
+        out_shape=[
+            jax.ShapeDtypeStruct(w_in.shape, F32),
+            jax.ShapeDtypeStruct(w_out.shape, F32),
+            jax.ShapeDtypeStruct((rows, chans), BF16),
+            jax.ShapeDtypeStruct((cells, chans), BF16),
+        ],
+        in_specs=[pl.BlockSpec((1, 2, 64, 16, 128), lambda i: (i, 0, 0, 0, 0)), slab(rows // NCH), slab(cells // NCH)],
+        out_specs=[pl.BlockSpec((chans, CH), lambda i: (0, i)), slab(CH), slab(rows // NCH), slab(cells // NCH)],
+        compiler_params=pltpu.CompilerParams(vmem_limit_bytes=60 * 2**20),
+        name="finish",
+    )(sums, nest_grad, parent_out)
+    return (parent_out.reshape(parent.shape), nest_grad.reshape(nest_state.shape), grad_in, grad_out)
 
 
 def solution(mesh):

time: 86.6 us -> 81.3 us (0.939)
  other arithmetic: 6.89 us -> 0 us
  Pallas kernels: 76.2 us -> 79.7 us
  local copies, waits for them, and re-layouts: 2.12 us -> 0 us
    pallas_call x0 -> x1, Pallas kernels: none -> 8.69 us  [local(): pl.pallas_call(finish_kernel, grid=(NCH,), out_shape=[jax.ShapeDtypeStruc...]
    convert_element_type x2 -> x0, other arithmetic: 6.89 us -> none  [the longest x1 4.28 us: local(): grad_in.astype(F32)]
    pallas_call x1, Pallas kernels: 76.2 us -> 71 us  [local(): pl.pallas_call(lambda *refs: step_kernel(factor, *refs), out_shape=[jax.S...]
    unnamed x8 -> x0, local copies, waits for them, and re-layouts: 2.12 us -> none
where the time goes in v3:
time: 81.3 us; the launch traced here: 81 us
  Pallas kernels  79.7 us (98%)
  between operations  1.29 us (2%)
    pallas_call x1, Pallas kernels, local(): pl.pallas_call(lambda *refs: step_kernel(factor, *refs), out_shape=[jax.S...  71 us
    pallas_call x1, Pallas kernels, local(): pl.pallas_call(finish_kernel, grid=(NCH,), out_shape=[jax.ShapeDtypeStruc...  8.69 us

profile of v3, /device:TPU:1, one launch (start us, length us, event | category | flops | bytes accessed | tf_op | source)
XLA Modules:
  0.0 81.0 jit_solution(8665483560312379973)
XLA Ops:
  1.3 71.0 %nest_step.1 = (bf16[512,512]{1,0:T(8,128)(2,1)}, bf16[2048,512]{1,0:T(8,128)(2,1)}, bf16[8,2,64,16,128]{4,3,2,1,0:T(8,128)(2,1)}) custom-call(s32[1]{0:T(128)S(6)} %copy.12.refs_0_, bf16[16,32,512]{2,1,0:T(8,128)(2,1)} %refs_1_.1, f32[1,512]{1,0:T(1,128)} %bitcast.8, bf16[2048,512]{1,0:T(8,128)(2,1)} %bitcast.6, bf16[2048,512]{1,0:T(8,128)(2,1)} %bitcast.7, ...), custom_call_target="tpu_custom_call" | custom-call | tf_op jit(solution)/shard_map/nest_step/pallas_call | solution.py:342
  72.3 8.7 %finish.1 = (f32[512,2048]{1,0:T(8,128)}, f32[2048,512]{1,0:T(8,128)}, bf16[2048,512]{1,0:T(8,128)(2,1)}, bf16[512,512]{1,0:T(8,128)(2,1)}) custom-call(bf16[8,2,64,16,128]{4,3,2,1,0:T(8,128)(2,1)} %get-tuple-element.11.sums, bf16[2048,512]{1,0:T(8,128)(2,1)} %get-tuple-element.12.dx_in, bf16[512,512]{1,0:T(8,128)(2,1)} %get-tuple-element.13.field_in), custom_call_target="tpu_custom_call" | custom-call | tf_op jit(solution)/shard_map/finish/pallas_call | solution.py:387

commit v4 on v3

--- a/solution.py
+++ b/solution.py
@@ -138,7 +138,8 @@
 
     def s6(self, c, sums, out):
         self.wait(self.full.at[c, 1 - self.at.core], 5, c)
-        pltpu.make_async_copy(self.full.at[c], sums.at[c], out.at[c]).start()
+        for m in range(2):
+            pltpu.make_async_copy(self.full.at[c, m], sums[m].at[c], out.at[c, m]).start()
 
     def drain(self, c):
         for stage, ref in enumerate((self.rc, self.ra, self.rp, self.rp, self.ra, self.rc)):
@@ -159,8 +160,8 @@
 
 def step_kernel(
     factor, count, parent_h, diff, nest_h, cot_h, pos, wi_h, wo_h,
-    pout, dx, sums,
-    ext, edge, beside, sm, x, xT, cot, wi, wo, da, act, dh, fb, field_out, load, out, hs, hr, part, *scratch,
+    pout, dx, sums_in, sums_out,
+    ext, edge, beside, sm, x, xT, cot, wi, wo, da, act, dh, fb, field_out, load, out, leaving, hs, hr, part, *scratch,
 ):
     r = Reduce(part, *scratch)
     at = r.at
@@ -278,7 +279,7 @@
                 stage(c)
 
     odd = ((r.s1, 1), (r.s3, 4), (r.s5, 7),)
-    even = ((r.s2, 2), (r.s4, 5), ((lambda c: r.s6(c, sums, out.at[pl.ds(8, NCH)])), 7),)
+    even = ((r.s2, 2), (r.s4, 5), ((lambda c: r.s6(c, (sums_in, sums_out), leaving)), 7),)
     tiles(0, True)
 
     def slot(s):
@@ -317,19 +318,18 @@
     def leave(t):
         rows = rows_of(t, 256)
         pltpu.make_async_copy(cot.at[rows], dx.at[rows], out.at[t]).wait()
-        pltpu.make_async_copy(r.full.at[t], sums.at[t], out.at[8 + t]).wait()
+        pltpu.make_async_copy(r.full.at[t, 0], sums_in.at[t], leaving.at[t, 0]).wait()
+        pltpu.make_async_copy(r.full.at[t, 1], sums_out.at[t], leaving.at[t, 1]).wait()
 
     every(8, leave)
     pltpu.make_async_copy(field_out, pout, out.at[16]).wait()
 
 
-def finish_kernel(sums, dx_in, field_in, gi, go, dx, field):
+def finish_kernel(sums_in, sums_out, gi, go):
     for k in range(2):
-        gi[:, 128 * k : 128 * k + 128] = sums[0, 0, 32 * k : 32 * k + 32].reshape(512, 128).astype(F32)
+        gi[:, 128 * k : 128 * k + 128] = sums_in[0, 32 * k : 32 * k + 32].reshape(512, 128).astype(F32)
     for k in range(4):
-        go[:, 128 * k : 128 * k + 128] = sums[0, 1, 16 * k : 16 * k + 16].reshape(256, 128).astype(F32)
-    dx[...] = dx_in[...]
-    field[...] = field_in[...]
+        go[:, 128 * k : 128 * k + 128] = sums_out[0, 16 * k : 16 * k + 16].reshape(256, 128).astype(F32)
 
 
 def local(parent, diffusion, nest_state, nest_cotangent, owner_count, tile_pos, w_in, w_out):
@@ -339,15 +339,16 @@
     devices = lax.axis_size(("lat", "lon"))
     factor = 1.0 / math.sqrt(own_tiles * devices // 4 * tile_rows)
     hbm = pl.BlockSpec(memory_space=pl.ANY)
-    parent_out, nest_grad, sums = pl.pallas_call(
+    parent_out, nest_grad, sums_in, sums_out = pl.pallas_call(
         lambda *refs: step_kernel(factor, *refs),
         out_shape=[
             jax.ShapeDtypeStruct((cells, chans), BF16),
             jax.ShapeDtypeStruct((rows, chans), BF16),
-            jax.ShapeDtypeStruct((NCH, 2, 64, 16, 128), BF16),
+            jax.ShapeDtypeStruct((NCH, 64, 16, 128), BF16),
+            jax.ShapeDtypeStruct((NCH, 64, 16, 128), BF16),
         ],
         in_specs=[pl.BlockSpec(memory_space=pltpu.SMEM), hbm, VMEM, hbm, hbm, VMEM, hbm, hbm],
-        out_specs=[hbm] * 3,
+        out_specs=[hbm] * 4,
         scratch_shapes=[
             pltpu.VMEM((blat + 2, blon, chans), BF16),
             pltpu.VMEM((2, blat, chans), F32),
@@ -365,6 +366,7 @@
             pltpu.VMEM((cells, chans), BF16),
             pltpu.SemaphoreType.DMA((5,)),
             pltpu.SemaphoreType.DMA((17,)),
+            pltpu.SemaphoreType.DMA((NCH, 2)),
             pltpu.SemaphoreType.DMA((4,)),
             pltpu.SemaphoreType.DMA((4,)),
             pltpu.VMEM((NCH, 2, 64, 16, 128), BF16),
@@ -384,20 +386,15 @@
         nest_cotangent.reshape(rows, chans), tile_pos.reshape(1, own_tiles), w_in, w_out,
     )
     slab = lambda n: pl.BlockSpec((n, chans), lambda i: (i, 0))
-    grad_in, grad_out, nest_grad, parent_out = pl.pallas_call(
+    grad_in, grad_out = pl.pallas_call(
         finish_kernel,
         grid=(NCH,),
-        out_shape=[
-            jax.ShapeDtypeStruct(w_in.shape, F32),
-            jax.ShapeDtypeStruct(w_out.shape, F32),
-            jax.ShapeDtypeStruct((rows, chans), BF16),
-            jax.ShapeDtypeStruct((cells, chans), BF16),
-        ],
-        in_specs=[pl.BlockSpec((1, 2, 64, 16, 128), lambda i: (i, 0, 0, 0, 0)), slab(rows // NCH), slab(cells // NCH)],
-        out_specs=[pl.BlockSpec((chans, CH), lambda i: (0, i)), slab(CH), slab(rows // NCH), slab(cells // NCH)],
-        compiler_params=pltpu.CompilerParams(vmem_limit_bytes=60 * 2**20),
+        out_shape=[jax.ShapeDtypeStruct(w_in.shape, F32), jax.ShapeDtypeStruct(w_out.shape, F32)],
+        in_specs=[pl.BlockSpec((1, 64, 16, 128), lambda i: (i, 0, 0, 0))] * 2,
+        out_specs=[pl.BlockSpec((chans, CH), lambda i: (0, i)), slab(CH)],
+        compiler_params=pltpu.CompilerParams(vmem_limit_bytes=8 * 2**20),
         name="finish",
-    )(sums, nest_grad, parent_out)
+    )(sums_in, sums_out)
     return (parent_out.reshape(parent.shape), nest_grad.reshape(nest_state.shape), grad_in, grad_out)
 
 

time: 81.3 us -> 82.3 us (1.012)
  local copies, waits for them, and re-layouts: 0 us -> 5.29 us
  Pallas kernels: 79.7 us -> 75.5 us
    unnamed x0 -> x10, local copies, waits for them, and re-layouts: none -> 5.29 us
    pallas_call x1, Pallas kernels: 8.69 us -> 4.39 us  [local(): pl.pallas_call(finish_kernel, grid=(NCH,), out_shape=[jax.ShapeDtypeStruc...]
where the time goes in v4:
time: 82.3 us; the launch traced here: 82.1 us
  Pallas kernels  75.5 us (92%)
  local copies, waits for them, and re-layouts  5.29 us (6%)
  between operations  1.3 us (2%)
    pallas_call x1, Pallas kernels, local(): pl.pallas_call(lambda *refs: step_kernel(factor, *refs), out_shape=[jax.S...  71.1 us
    unnamed x10, local copies, waits for them, and re-layouts  5.29 us
    pallas_call x1, Pallas kernels, local(): pl.pallas_call(finish_kernel, grid=(NCH,), out_shape=[jax.ShapeDtypeStruc...  4.39 us

profile of v4, /device:TPU:1, one launch (start us, length us, event | category | flops | bytes accessed | tf_op | source)
XLA Modules:
  0.0 82.1 jit_solution(819360256789768774)
XLA Ops:
  1.3 71.1 %nest_step.1 = (bf16[512,512]{1,0:T(8,128)(2,1)}, bf16[2048,512]{1,0:T(8,128)(2,1)}, bf16[8,64,16,128]{3,2,1,0:T(8,128)(2,1)}, bf16[8,64,16,128]{3,2,1,0:T(8,128)(2,1)}) custom-call(s32[1]{0:T(128)S(6)} %copy.14.refs_0_, bf16[16,32,512]{2,1,0:T(8,128)(2,1)} %refs_1_.1, f32[1,512]{1,0:T(1,128)} %bitcast.10, bf16[2048,512]{1,0:T(8,128)(2,1)} %bitcast.7, ...), custom_call_target="tpu_custom_call" | custom-call | tf_op jit(solution)/shard_map/nest_step/pallas_call | solution.py:342
  72.4 0.0 copy-start
  72.4 1.6 %copy-done = bf16[8,64,16,128]{3,2,1,0:T(8,128)(2,1)S(1)} copy-done((bf16[8,64,16,128]{3,2,1,0:T(8,128)(2,1)S(1)}, bf16[8,64,16,128]{3,2,1,0:T(8,128)(2,1)}, u32[]{:S(2)}) %copy-start) | copy-done | bytes 2097176
  74.0 0.0 copy-start.1
  74.0 1.6 %copy-done.1 = bf16[8,64,16,128]{3,2,1,0:T(8,128)(2,1)S(1)} copy-done((bf16[8,64,16,128]{3,2,1,0:T(8,128)(2,1)S(1)}, bf16[8,64,16,128]{3,2,1,0:T(8,128)(2,1)}, u32[]{:S(2)}) %copy-start.1) | copy-done | bytes 2097176
  75.6 0.0 copy-start.3
  75.6 0.0 copy-start.2
  75.6 4.4 %finish.1 = (f32[512,2048]{1,0:T(8,128)}, f32[2048,512]{1,0:T(8,128)}) custom-call(bf16[8,64,16,128]{3,2,1,0:T(8,128)(2,1)S(1)} %copy-done, bf16[8,64,16,128]{3,2,1,0:T(8,128)(2,1)S(1)} %copy-done.1), custom_call_target="tpu_custom_call" | custom-call | tf_op jit(solution)/shard_map/finish/pallas_call | solution.py:389
  80.0 0.0 copy-done.3
  80.0 0.8 copy.15
  80.8 0.0 copy-done.2
  80.8 1.3 %copy.16 = bf16[256,8,512]{2,1,0:T(8,128)(2,1)} copy(bf16[256,8,512]{2,1,0:T(8,128)(2,1)S(1)} %bitcast.6) | data formatting | bytes 4194304
Async XLA Ops:
  72.4 1.6 %copy-start = (bf16[8,64,16,128]{3,2,1,0:T(8,128)(2,1)S(1)}, bf16[8,64,16,128]{3,2,1,0:T(8,128)(2,1)}, u32[]{:S(2)}) copy-start(bf16[8,64,16,128]{3,2,1,0:T(8,128)(2,1)} %get-tuple-element.12.sums_in) | copy-start | bytes 6291460
  74.0 1.6 %copy-start.1 = (bf16[8,64,16,128]{3,2,1,0:T(8,128)(2,1)S(1)}, bf16[8,64,16,128]{3,2,1,0:T(8,128)(2,1)}, u32[]{:S(2)}) copy-start(bf16[8,64,16,128]{3,2,1,0:T(8,128)(2,1)} %get-tuple-element.13.sums_out) | copy-start | bytes 6291460
  75.6 4.4 %copy-start.3 = (bf16[512,512]{1,0:T(8,128)(2,1)S(1)}, bf16[512,512]{1,0:T(8,128)(2,1)}, u32[]{:S(2)}) copy-start(bf16[512,512]{1,0:T(8,128)(2,1)} %get-tuple-element.10) | copy-start | bytes 1572868
  75.6 5.2 %copy-start.2 = (bf16[2048,512]{1,0:T(8,128)(2,1)S(1)}, bf16[2048,512]{1,0:T(8,128)(2,1)}, u32[]{:S(2)}) copy-start(bf16[2048,512]{1,0:T(8,128)(2,1)} %get-tuple-element.11) | copy-start | bytes 6291460
